TPU v7x, 32 devices: a whole 2x2x4 slice. The times are simulated.
32 devices in a mesh: seq: 4 (over z), head: 2 (over y), dp: 4 (over x, core).
Axes of the slice: x: 2, y: 2, z: 4, core: 2. Of those that a mesh axis runs over, the one named last changes fastest.
Arguments:
- layer_input: bfloat16 [4, 512, 6144], P('dp', 'seq'), may hold values from -6 to 6
- queries: bfloat16 [4, 512, 1024], P('dp', 'seq', 'head'), may hold values from -6 to 6
- key_rows: bfloat16 [4, 512, 1024], P('dp', 'seq', 'head'), may hold values from -6 to 6
- value_rows: bfloat16 [4, 512, 1024], P('dp', 'seq', 'head'), may hold values from -6 to 6
- grad_out: bfloat16 [4, 512, 1024], P('dp', 'seq', 'head'), may hold values from -6 to 6
- log_decay: float32 [4, 512, 8], P('dp', 'seq', 'head'), may hold values from -2 to 0, as said below
Outputs:
- grad_query: bfloat16 [4, 512, 1024], P('dp', 'seq', 'head')
- grad_key: bfloat16 [4, 512, 1024], P('dp', 'seq', 'head')
- grad_value: bfloat16 [4, 512, 1024], P('dp', 'seq', 'head')
- key_weight_grad: bfloat16 [6144, 1024], P('seq', 'head')
- value_weight_grad: bfloat16 [6144, 1024], P('seq', 'head')
Inputs may be any that keep to these rules, and one draw needn't show every extreme that they name: log_decay is never positive.
All inputs are finite; a program needn't handle non-finite values.
Results may differ from a plain program's by a relative error of at most 0.0062.
Values may be sent and summed in bfloat16 or wider, within the bound.
A program may use at most 64 MiB of HBM per device.

v0:
```python
import math
import jax
import jax.numpy as jnp
from jax import lax
from jax.sharding import PartitionSpec as P

DH = 128
top_precision = lax.Precision.HIGHEST


def per_device(layer_input, queries, key_rows, value_rows, grad_out, log_decay):
    length = queries.shape[1]
    heads = log_decay.shape[2]
    query_three = queries[0].reshape(length, heads, DH)
    key_three = key_rows[0].reshape(length, heads, DH)
    triple_value = value_rows[0].reshape(length, heads, DH)
    triple_gradient = grad_out[0].reshape(length, heads, DH)
    running = jnp.cumsum(log_decay[0], axis=0)
    totals = running[-1]
    across = running.T
    positions = jnp.arange(length)
    lower_mask = positions[:, None] >= positions[None, :]
    decay_mask = jnp.where(
        lower_mask[None], jnp.exp(jnp.minimum(across[:, :, None] - across[:, None, :], 0.0)), 0.0
    )
    to_end = jnp.exp(totals[None, :] - running)
    from_start = jnp.exp(running)
    key_rows_scaled = (key_three * to_end[:, :, None]).astype(jnp.bfloat16)
    scaled_queries = (query_three * from_start[:, :, None]).astype(jnp.bfloat16)
    key_state = jnp.einsum(
        "nrx,nro->rxo", key_rows_scaled, triple_value, preferred_element_type=jnp.float32
    )
    query_state = jnp.einsum(
        "thq,thv->hqv", scaled_queries, triple_gradient, preferred_element_type=jnp.float32
    )
    every_key_row, all_queries, all_totals = (
        lax.all_gather(key_state[None], "seq", axis=0, tiled=True),
        lax.all_gather(query_state[None], "seq", axis=0, tiled=True),
        lax.all_gather(totals[None], "seq", axis=0, tiled=True),
    )
    count = lax.axis_size("seq")
    here = lax.axis_index("seq")
    through = jnp.cumsum(all_totals, axis=0)
    before = through - all_totals
    block_ids = jnp.arange(count)[:, None]
    own_before = lax.dynamic_index_in_dim(before, here, 0, keepdims=False)
    own_through = lax.dynamic_index_in_dim(through, here, 0, keepdims=False)
    leading_weight = jnp.where(
        block_ids < here, jnp.exp(jnp.minimum(own_before[None] - through, 0.0)), 0.0
    )
    late_weight = jnp.where(
        block_ids > here, jnp.exp(jnp.minimum(before - own_through[None], 0.0)), 0.0
    )
    prefix_running = jnp.einsum(
        "cp,cpqt->pqt", leading_weight, every_key_row, precision=top_precision
    )
    suffix = jnp.einsum("nh,nhqv->hqv", late_weight, all_queries, precision=top_precision)
    prefix_reduced = prefix_running.astype(jnp.bfloat16)
    suffix_low = suffix.astype(jnp.bfloat16)
    value_scores = jnp.einsum(
        "thv,jhv->htj", triple_gradient, triple_value, preferred_element_type=jnp.float32
    )
    value_weights = (value_scores * decay_mask).astype(jnp.bfloat16)
    key_scores = jnp.einsum(
        "thq,jhq->htj", query_three, key_three, preferred_element_type=jnp.float32
    )
    key_weights = (key_scores * decay_mask).astype(jnp.bfloat16)
    scale = 1.0 / DH
    query_grad = (
        jnp.einsum("htj,jhk->thk", value_weights, key_three, preferred_element_type=jnp.float32)
        + from_start[:, :, None]
        * jnp.einsum(
            "jfg,xjg->xjf", prefix_reduced, triple_gradient, preferred_element_type=jnp.float32
        )
    ) * scale
    key_grad = (
        jnp.einsum("htj,thq->jhq", value_weights, query_three, preferred_element_type=jnp.float32)
        + to_end[:, :, None]
        * jnp.einsum("hqv,jhv->jhq", suffix_low, triple_value, preferred_element_type=jnp.float32)
    ) * scale
    value_grad = (
        jnp.einsum("htj,thv->jhv", key_weights, triple_gradient, preferred_element_type=jnp.float32)
        + to_end[:, :, None]
        * jnp.einsum("hqv,jhq->jhv", suffix_low, key_three, preferred_element_type=jnp.float32)
    ) * scale
    grad_query = query_grad.astype(jnp.bfloat16).reshape(1, length, heads * DH)
    grad_key = key_grad.astype(jnp.bfloat16).reshape(1, length, heads * DH)
    grad_value = value_grad.astype(jnp.bfloat16).reshape(1, length, heads * DH)
    columns = lax.all_to_all(layer_input, "seq", split_axis=2, concat_axis=1, tiled=True)
    rows = columns[0]
    dims = (((0,), (0,)), ((), ()))
    key_part = lax.dot_general(
        rows,
        lax.all_gather(grad_key, "seq", axis=1, tiled=True)[0],
        dims,
        preferred_element_type=jnp.float32,
    )
    value_part = lax.dot_general(
        rows,
        lax.all_gather(grad_value, "seq", axis=1, tiled=True)[0],
        dims,
        preferred_element_type=jnp.float32,
    )
    factor = 1.0 / math.sqrt(lax.axis_size("dp") * lax.axis_size("seq") * layer_input.shape[1])
    key_summed, value_summed = lax.psum((key_part, value_part), "dp")
    key_weight_grad = (key_summed * factor).astype(jnp.bfloat16)
    value_weight_grad = (value_summed * factor).astype(jnp.bfloat16)
    return (grad_query, grad_key, grad_value, key_weight_grad, value_weight_grad)


def solution(mesh):
    return jax.shard_map(
        per_device,
        mesh=mesh,
        in_specs=(
            P("dp", "seq", None),
            P("dp", "seq", "head"),
            P("dp", "seq", "head"),
            P("dp", "seq", "head"),
            P("dp", "seq", "head"),
            P("dp", "seq", "head"),
        ),
        out_specs=(
            P("dp", "seq", "head"),
            P("dp", "seq", "head"),
            P("dp", "seq", "head"),
            P("seq", "head"),
            P("seq", "head"),
        ),
        check_vma=False,
    )
```

profile of v0, /device:TPU:0, one launch (start us, length us, event | category | flops | bytes accessed | tf_op | source)
XLA Modules:
  0.0 296.4 jit_solution(7479897676144758266)
XLA Ops:
  7.2 0.8 copy.80
  8.3 1.0 copy.88
  9.3 1.0 copy.119
  10.4 0.9 fusion.19
  11.3 6.8 %copy.96 = bf16[1,128,6144]{1,0,2:T(2,128)(2,1)S(1)} copy(bf16[1,128,6144]{2,1,0:T(8,128)(2,1)} %param.6) | data formatting | bytes 3145728 | tf_op args[0]
  18.2 0.5 broadcast.43
  18.7 34.4 %reduce.2 = bf16[6144,128]{1,0:T(8,128)(2,1)} reduce(bf16[6144,1,128]{2,1,0:T(2,128)(2,1)S(1)} %bitcast.97, bf16[]{:T(256)} %broadcast.43), dimensions={1}, to_apply=%bitcast.77.reduce_sub_computation | reduce | bytes 3145730
  53.1 3.7 %reshape.75 = bf16[4,2,98304]{2,1,0:T(2,128)(2,1)} reshape(bf16[6144,128]{1,0:T(8,128)(2,1)} %reduce.2) | data formatting | bytes 3145728
  56.8 6.5 %all-to-all-start = ((bf16[4,2,98304]{2,1,0:T(2,128)(2,1)}), bf16[4,2,98304]{2,1,0:T(2,128)(2,1)}, u32[]{:S(2)}, u32[]{:S(2)}) async-start(bf16[4,2,98304]{2,1,0:T(2,128)(2,1)} %reshape.75), calls=%async_computation | async-start | bytes 3145728 | tf_op jit(solution)/shard_map/all_to_all | solution.py:89
  63.5 0.9 fusion.18
  64.5 44.7 %all-gather.2 = f32[4,1,4]{2,1,0:T(1,128)S(1)} all-gather(f32[1,1,4]{2,1,0:T(1,128)S(1)} %get-tuple-element.32), channel_id=1, replica_groups=mesh['seq'=4,'head'=2,'dp'=4] {'seq'}, dimensions={0}, use_global_device_ids=true | all-gather | bytes 80 | tf_op jit(solution)/shard_map/all_gather | solution.py:39
  109.4 0.2 fusion.12
  109.7 1.4 multiply_reduce_fusion
  111.2 0.2 fusion.5
  111.6 23.9 %all_gather.18 = bf16[1,512,512]{1,2,0:T(8,128)(2,1)} all-gather(bf16[1,128,512]{1,2,0:T(8,128)(2,1)S(1)} %bitcast.104), channel_id=1, replica_groups=mesh['seq'=4,'head'=2,'dp'=4] {'seq'}, dimensions={1}, use_global_device_ids=true | all-gather | bytes 655360 | tf_op jit(solution)/shard_map/all_gather | solution.py:94
  135.7 0.4 fusion.11
  136.1 14.7 %all_gather.19 = bf16[1,512,512]{1,2,0:T(8,128)(2,1)} all-gather(bf16[1,128,512]{1,2,0:T(8,128)(2,1)S(1)} %bitcast.117), channel_id=1, replica_groups=mesh['seq'=4,'head'=2,'dp'=4] {'seq'}, dimensions={1}, use_global_device_ids=true | all-gather | bytes 655360 | tf_op jit(solution)/shard_map/all_gather | solution.py:100
  150.8 3.1 %reshape.76 = bf16[6144,1,128]{2,1,0:T(2,128)(2,1)S(1)} reshape(bf16[4,2,98304]{2,1,0:T(2,128)(2,1)} %all-to-all-done) | data formatting | bytes 3145728
  153.8 1.3 copy.117
  155.2 1.8 copy.97
  157.0 2.6 convolution_bitcast_fusion
  159.6 2.6 convolution_bitcast_fusion.1
  162.5 0.7 copy-done.10
  163.4 0.8 copy.100
  164.1 0.8 copy.99
  164.9 3.6 %fusion.14 = f32[4,1,128,128]{3,1,2,0:T(1,128)S(1)} fusion(f32[4,4,1,1]{0,2,3,1:T(1,128)S(1)} %copy.103, f32[4,4,128,128]{3,2,1,0:T(8,128)} %bitcast.114), kind=kOutput, calls=%fused_computation.27 | convolution fusion | flops 3145728 | bytes 1310784 | tf_op jit(solution)/shard_map/cp,cpqt->pqt/dot_general | solution.py:54
  168.7 0.8 copy.98
  169.5 112.8 %all-reduce.3.cloned.1.call-done = (f32[1536,512]{0,1:T(8,128)}, f32[1536,512]{0,1:T(8,128)}) async-done(((f32[1536,512]{0,1:T(8,128)}, f32[1536,512]{0,1:T(8,128)}), (f32[1536,512]{0,1:T(8,128)}, f32[1536,512]{0,1:T(8,128)})) %all-reduce.3.cloned.1.call-update) | async-done | bytes 6291472 | tf_op jit(solution)/shard_map/psum | solution.py:105
  282.2 2.2 multiply_convert_fusion.1
  284.5 1.6 copy.101
  286.0 2.2 multiply_convert_fusion
  288.3 1.6 copy.102
  (55 shorter events, 1.9 us)
Async XLA Ops:
  7.2 102.5 %all-gather.8.cloned.1.call-start = ((), (), s32[]{:S(2)}) async-start(), calls=%async_computation.2 | async-start | bytes 1310720 | tf_op jit(solution)/shard_map/all_gather | solution.py:38
  8.2 10.0 %copy-start.5 = (f32[128,4]{1,0:T(8,128)}, f32[128,4]{1,0:T(8,128)S(1)}, u32[]{:S(2)}) copy-start(f32[128,4]{1,0:T(8,128)S(1)} %reduce_window_sum.22) | copy-start | bytes 6148
  10.4 99.0 %copy-start.2 = (bf16[1,128,512]{1,2,0:T(8,128)(2,1)}, bf16[1,128,512]{1,2,0:T(8,128)(2,1)S(1)}, u32[]{:S(2)}) copy-start(bf16[1,128,512]{1,2,0:T(8,128)(2,1)S(1)} %copy.119) | copy-start | bytes 393220
  56.8 6.5 %copy-start.11 = (bf16[1,128,512]{2,1,0:T(8,128)(2,1)S(1)}, bf16[1,128,512]{2,1,0:T(8,128)(2,1)}, u32[]{:S(2)}) copy-start(bf16[1,128,512]{2,1,0:T(8,128)(2,1)} %param.9) | copy-start | bytes 393220
  56.8 6.6 %copy-start.12 = (bf16[1,128,512]{2,1,0:T(8,128)(2,1)S(1)}, bf16[1,128,512]{2,1,0:T(8,128)(2,1)}, u32[]{:S(2)}) copy-start(bf16[1,128,512]{2,1,0:T(8,128)(2,1)} %param.8) | copy-start | bytes 393220
  56.8 52.3 %copy-start.6 = (f32[128,4]{1,0:T(8,128)S(1)}, f32[128,4]{1,0:T(8,128)}, u32[]{:S(2)}) copy-start(f32[128,4]{1,0:T(8,128)} %copy-done.5) | copy-start | bytes 6148
  56.8 94.0 %all-to-all-start = ((bf16[4,2,98304]{2,1,0:T(2,128)(2,1)}), bf16[4,2,98304]{2,1,0:T(2,128)(2,1)}, u32[]{:S(2)}, u32[]{:S(2)}) async-start(bf16[4,2,98304]{2,1,0:T(2,128)(2,1)} %reshape.75), calls=%async_computation | async-start | bytes 3145728 | tf_op jit(solution)/shard_map/all_to_all | solution.py:89
  63.3 101.6 %all-gather.6.cloned.1.call-start = ((), (), s32[]{:S(2)}) async-start(), calls=%async_computation.1 | async-start | bytes 1310720 | tf_op jit(solution)/shard_map/all_gather | solution.py:37
  64.4 217.8 %all-reduce.3.cloned.1.call-start = ((), (), s32[]{:S(2)}) async-start(), calls=%async_computation.3 | async-start | bytes 12582912 | tf_op jit(solution)/shard_map/psum | solution.py:105
  109.6 25.9 %copy-start.9 = (bf16[4,128,128]{2,1,0:T(8,128)(2,1)}, bf16[4,128,128]{2,1,0:T(8,128)(2,1)S(1)}, u32[]{:S(2)}) copy-start(bf16[4,128,128]{2,1,0:T(8,128)(2,1)S(1)} %fusion.12) | copy-start | bytes 393220
  111.1 24.7 %copy-start.3 = (bf16[1,128,512]{1,2,0:T(8,128)(2,1)S(1)}, bf16[1,128,512]{1,2,0:T(8,128)(2,1)}, u32[]{:S(2)}) copy-start(bf16[1,128,512]{1,2,0:T(8,128)(2,1)} %copy-done.2) | copy-start | bytes 393220
  136.1 14.7 %copy-start.7 = (bf16[128,4,128]{0,2,1:T(8,128)(2,1)}, bf16[128,4,128]{0,2,1:T(8,128)(2,1)S(1)}, u32[]{:S(2)}) copy-start(bf16[128,4,128]{0,2,1:T(8,128)(2,1)S(1)} %fusion.11) | copy-start | bytes 393220
  155.2 1.8 copy-start.1
  157.0 2.6 copy-start
  162.3 0.9 copy-start.10
  162.3 1.1 copy-start.8
  162.3 6.2 %copy-start.4 = (bf16[1,128,512]{1,2,0:T(8,128)(2,1)S(1)}, bf16[1,128,512]{1,2,0:T(8,128)(2,1)}, u32[]{:S(2)}) copy-start(bf16[1,128,512]{1,2,0:T(8,128)(2,1)} %copy-done.2) | copy-start | bytes 393220
Sparse Core Ops, SparseCore 0:
  11.4 30.6 all-gather.7
  65.7 45.5 all-gather.5
  162.4 119.7 all-reduce.2
where the time goes:
time: 297 us; the launch traced here: 296 us
  waiting for transfers between devices  113 us (38%)
  blocking collectives  83.2 us (28%)
  other arithmetic  40.7 us (14%)
  local copies, waits for them, and re-layouts  26.9 us (9%)
  between operations  14 us (5%)
  matrix products  12.2 us (4%)
  starting transfers between devices  6.54 us (2%)
    psum x1, waiting for transfers between devices, per_device(): key_summed, value_summed = lax.psum((key_part, value_part), 'dp')  113 us
    all_gather x1, blocking collectives, per_device(): lax.all_gather(totals[None], 'seq', axis=0, tiled=True)  44.7 us
    unnamed x3, other arithmetic  35.9 us
    all_gather x1, blocking collectives, per_device(): lax.all_gather(grad_key, 'seq', axis=1, tiled=True)[0]  23.9 us
    unnamed x38, local copies, waits for them, and re-layouts  22.8 us
    all_gather x1, blocking collectives, per_device(): lax.all_gather(grad_value, 'seq', axis=1, tiled=True)[0]  14.7 us
    all_to_all x1, starting transfers between devices, per_device(): lax.all_to_all(layer_input, 'seq', split_axis=2, concat_axis=1, tiled=True)  6.46 us
  transfers between devices with their start and end apart: 4, of which 1 were waited for; matrix products, arithmetic and copies ran while one was open for 23% of the time, Pallas kernels for 0%

commit v1 on v0

--- a/solution.py
+++ b/solution.py
@@ -6,6 +6,12 @@
 
 DH = 128
 top_precision = lax.Precision.HIGHEST
+_link_members_all = lambda m: jnp.concatenate(
+    lax.all_to_all(
+        jnp.stack(jnp.split(m, lax.axis_size("seq"), axis=2)), "seq", split_axis=0, concat_axis=0
+    ),
+    axis=1,
+)
 
 
 def per_device(layer_input, queries, key_rows, value_rows, grad_out, log_decay):
@@ -86,7 +92,7 @@
     grad_query = query_grad.astype(jnp.bfloat16).reshape(1, length, heads * DH)
     grad_key = key_grad.astype(jnp.bfloat16).reshape(1, length, heads * DH)
     grad_value = value_grad.astype(jnp.bfloat16).reshape(1, length, heads * DH)
-    columns = lax.all_to_all(layer_input, "seq", split_axis=2, concat_axis=1, tiled=True)
+    columns = _link_members_all(layer_input)
     rows = columns[0]
     dims = (((0,), (0,)), ((), ()))
     key_part = lax.dot_general(

time: 297 us -> 255 us (0.86)
  other arithmetic: 40.7 us -> 8.33 us
  local copies, waits for them, and re-layouts: 26.9 us -> 6.01 us
  blocking collectives: 83.2 us -> 95.3 us
    unnamed x3 -> x2, other arithmetic: 35.9 us -> 1.43 us
    unnamed x38 -> x13, local copies, waits for them, and re-layouts: 22.8 us -> 3.49 us
    all_gather x1, blocking collectives: 23.9 us -> 32.7 us  [per_device(): lax.all_gather(grad_key, 'seq', axis=1, tiled=True)[0]]
  transfers between devices with their start and end apart: 4 -> 4, of which waited for: 1 -> 1; matrix products, arithmetic and copies ran while one was open for 23% -> 7% of each run, Pallas kernels for 0% -> 0%
where the time goes in v1:
time: 255 us
  waiting for transfers between devices  113 us (44%)
  blocking collectives  95.3 us (37%)
  between operations  13.9 us (5%)
  matrix products  12.4 us (5%)
  other arithmetic  8.33 us (3%)
  starting transfers between devices  6.53 us (3%)
  local copies, waits for them, and re-layouts  6.01 us (2%)
    psum x1, waiting for transfers between devices, per_device(): key_summed, value_summed = lax.psum((key_part, value_part), 'dp')  113 us
    all_gather x1, blocking collectives, per_device(): lax.all_gather(totals[None], 'seq', axis=0, tiled=True)  46.9 us
    all_gather x1, blocking collectives, per_device(): lax.all_gather(grad_key, 'seq', axis=1, tiled=True)[0]  32.7 us
    all_gather x1, blocking collectives, per_device(): lax.all_gather(grad_value, 'seq', axis=1, tiled=True)[0]  15.7 us
    all_to_all x1, starting transfers between devices, lax.all_to_all(jnp.stack(jnp.split(m, lax.axis_size('seq'), axis=2)), 'se...  6.45 us
  transfers between devices with their start and end apart: 4, of which 1 were waited for; matrix products, arithmetic and copies ran while one was open for 7% of the time, Pallas kernels for 0%

profile of v1, /device:TPU:0, one launch (start us, length us, event | category | flops | bytes accessed | tf_op | source)
XLA Modules:
  0.0 255.1 jit_solution(13802505923629396627)
XLA Ops:
  7.2 0.9 copy.32
  8.1 0.2 reduce_window_sum.22
  8.4 1.0 copy.40
  9.4 1.0 copy.62
  10.5 0.9 fusion.21
  11.4 0.1 slice_bitcast_fusion.3
  11.6 1.3 pad_maximum_fusion
  12.9 6.4 %all-to-all-start = ((bf16[4,1,128,1536]{3,2,1,0:T(8,128)(2,1)}), bf16[4,1,128,1536]{3,2,1,0:T(8,128)(2,1)S(1)}, u32[]{:S(2)}, u32[]{:S(2)}) async-start(bf16[4,1,128,1536]{3,2,1,0:T(8,128)(2,1)} %pad_maximum_fusion), calls=%async_computation | async-start | bytes 3145728 | tf_op jit(solution)/shard_map/all_to_all | solution.py:10
  19.5 0.1 copy.35
  19.6 0.9 fusion.20
  20.6 46.9 %all-gather.2 = f32[4,1,4]{2,1,0:T(1,128)S(1)} all-gather(f32[1,1,4]{2,1,0:T(1,128)S(1)} %get-tuple-element.26), channel_id=1, replica_groups=mesh['seq'=4,'head'=2,'dp'=4] {'seq'}, dimensions={0}, use_global_device_ids=true | all-gather | bytes 80 | tf_op jit(solution)/shard_map/all_gather | solution.py:45
  67.6 0.2 fusion.12
  67.9 1.4 multiply_reduce_fusion
  69.3 0.1 copy.58
  69.4 0.2 fusion.5
  69.7 0.2 fusion.10
  69.9 32.7 %all_gather.18 = bf16[1,512,512]{1,2,0:T(8,128)(2,1)S(1)} all-gather(bf16[1,128,512]{1,2,0:T(8,128)(2,1)S(1)} %bitcast.100), channel_id=1, replica_groups=mesh['seq'=4,'head'=2,'dp'=4] {'seq'}, dimensions={1}, use_global_device_ids=true | all-gather | bytes 655360 | tf_op jit(solution)/shard_map/all_gather | solution.py:100
  102.6 0.2 fusion.4
  102.8 0.4 fusion.11
  103.2 15.7 %all_gather.19 = bf16[1,512,512]{1,2,0:T(8,128)(2,1)S(1)} all-gather(bf16[1,128,512]{1,2,0:T(8,128)(2,1)S(1)} %bitcast.113), channel_id=1, replica_groups=mesh['seq'=4,'head'=2,'dp'=4] {'seq'}, dimensions={1}, use_global_device_ids=true | all-gather | bytes 655360 | tf_op jit(solution)/shard_map/all_gather | solution.py:106
  118.9 2.7 %fusion.16 = f32[1536,512]{1,0:T(8,128)} fusion(bf16[512,1536]{1,0:T(8,128)(2,1)S(1)} %bitcast.94, bf16[1,512,512]{1,2,0:T(8,128)(2,1)S(1)} %all_gather.19), kind=kOutput, calls=%fused_computation.28 | convolution fusion | flops 805306368 | bytes 5242880 | tf_op jit(solution)/shard_map/dot_general | solution.py:104
  121.6 2.8 %fusion.18 = f32[1536,512]{1,0:T(8,128)} fusion(bf16[512,1536]{1,0:T(8,128)(2,1)S(1)} %bitcast.95, bf16[1,512,512]{1,2,0:T(8,128)(2,1)S(1)} %all_gather.18), kind=kOutput, calls=%fused_computation.30 | convolution fusion | flops 805306368 | bytes 5242880 | tf_op jit(solution)/shard_map/dot_general | solution.py:98
  124.4 0.1 copy.49
  124.5 0.2 convolution_bitcast_fusion.5
  124.7 0.8 copy.48
  125.5 0.8 copy.47
  126.3 3.6 %fusion.14 = f32[4,1,128,128]{3,1,2,0:T(1,128)S(1)} fusion(f32[4,4,1,1]{0,2,3,1:T(1,128)S(1)} %copy.49, f32[4,4,128,128]{3,2,1,0:T(8,128)} %bitcast.110), kind=kOutput, calls=%fused_computation.26 | convolution fusion | flops 3145728 | bytes 1310784 | tf_op jit(solution)/shard_map/cp,cpqt->pqt/dot_general | solution.py:60
  129.9 0.2 fusion.9
  130.0 0.8 copy.46
  130.8 112.5 %all-reduce.3.cloned.1.call-done = (f32[1536,512]{1,0:T(8,128)}, f32[1536,512]{1,0:T(8,128)}) async-done(((f32[1536,512]{1,0:T(8,128)}, f32[1536,512]{1,0:T(8,128)}), (f32[1536,512]{1,0:T(8,128)}, f32[1536,512]{1,0:T(8,128)})) %all-reduce.3.cloned.1.call-update) | async-done | bytes 6291472 | tf_op jit(solution)/shard_map/psum | solution.py:111
  243.4 3.6 %multiply_convert_fusion.1 = bf16[1536,512]{1,0:T(8,128)(2,1)} fusion(f32[1536,512]{1,0:T(8,128)} %get-tuple-element.15), kind=kLoop, calls=%fused_computation.1 | loop fusion | flops 1572864 | bytes 4718592 | tf_op jit(solution)/shard_map/convert_element_type | solution.py:112
  247.0 1.6 multiply_convert_fusion
  (30 shorter events, 0.7 us)
Async XLA Ops:
  7.2 4.2 %copy-start.1 = (bf16[1,128,6144]{2,1,0:T(8,128)(2,1)S(1)}, bf16[1,128,6144]{2,1,0:T(8,128)(2,1)}, u32[]{:S(2)}) copy-start(bf16[1,128,6144]{2,1,0:T(8,128)(2,1)} %param.6) | copy-start | bytes 4718596
  7.2 60.7 %all-gather.8.cloned.1.call-start = ((), (), s32[]{:S(2)}) async-start(), calls=%async_computation.2 | async-start | bytes 1310720 | tf_op jit(solution)/shard_map/all_gather | solution.py:44
  12.9 6.5 %copy-start.2 = (bf16[1,128,512]{2,1,0:T(8,128)(2,1)S(1)}, bf16[1,128,512]{2,1,0:T(8,128)(2,1)}, u32[]{:S(2)}) copy-start(bf16[1,128,512]{2,1,0:T(8,128)(2,1)} %param.9) | copy-start | bytes 393220
  12.9 6.6 %copy-start.3 = (bf16[1,128,512]{2,1,0:T(8,128)(2,1)S(1)}, bf16[1,128,512]{2,1,0:T(8,128)(2,1)}, u32[]{:S(2)}) copy-start(bf16[1,128,512]{2,1,0:T(8,128)(2,1)} %param.8) | copy-start | bytes 393220
  12.9 106.0 %all-to-all-start = ((bf16[4,1,128,1536]{3,2,1,0:T(8,128)(2,1)}), bf16[4,1,128,1536]{3,2,1,0:T(8,128)(2,1)S(1)}, u32[]{:S(2)}, u32[]{:S(2)}) async-start(bf16[4,1,128,1536]{3,2,1,0:T(8,128)(2,1)} %pad_maximum_fusion), calls=%async_computation | async-start | bytes 3145728 | tf_op jit(solution)/shard_map/all_to_all | solution.py:10
  19.3 106.9 %all-gather.6.cloned.1.call-start = ((), (), s32[]{:S(2)}) async-start(), calls=%async_computation.1 | async-start | bytes 1310720 | tf_op jit(solution)/shard_map/all_gather | solution.py:43
  20.5 222.8 %all-reduce.3.cloned.1.call-start = ((), (), s32[]{:S(2)}) async-start(), calls=%async_computation.3 | async-start | bytes 12582912 | tf_op jit(solution)/shard_map/psum | solution.py:111
  243.4 3.6 %copy-start = (f32[1536,512]{1,0:T(8,128)S(1)}, f32[1536,512]{1,0:T(8,128)}, u32[]{:S(2)}) copy-start(f32[1536,512]{1,0:T(8,128)} %get-tuple-element.16) | copy-start | bytes 9437188
Sparse Core Ops, SparseCore 0:
  11.5 54.5 all-gather.7
  68.3 37.9 all-gather.5
  124.5 118.8 all-reduce.2
